TPU v7x, 32 devices: a whole 2x2x4 slice. The times are simulated.
32 devices in a mesh: groups: 2 (over y), seq: 4 (over z), tensor: 2 (over x), sub: 2 (over core).
Axes of the slice: x: 2, y: 2, z: 4, core: 2. Of those that a mesh axis runs over, the one named last changes fastest.
Arguments:
- activations: bfloat16 [4096, 4096], P(('groups', 'seq'), ('tensor', 'sub')), parts along dimension 0, may hold values from -18 to 18
- conv_weight: bfloat16 [512, 4096], P(None, ('tensor', 'sub')), may hold values from -0.25 to 0.25
- query_weight: bfloat16 [4096, 2048], P('seq', ('tensor', 'sub')), may hold values from -0.09375 to 0.09375
- key_weight: bfloat16 [4096, 2048], P('seq', ('tensor', 'sub')), may hold values from -0.09375 to 0.09375
- value_weight: bfloat16 [4096, 2048], P('seq', ('tensor', 'sub')), may hold values from -0.09375 to 0.09375
- segment_for_slot: int32 [16], P('groups'), parts along dimension 0, may hold values from 0 to 7, each once
- book_length: int32 [2], P('groups'), parts along dimension 0, may hold values from 1024 to 2048
Outputs:
- context: bfloat16 [4096, 2048], P(('groups', 'seq'), ('tensor', 'sub')), parts along dimension 0
There are 2 independent parts, one for each index of `groups`. A program takes and returns all parts, laid end to end along the dimension named above; an argument that names none is the same for every part. Nothing has to cross between parts.
Inputs may be any that keep to these rules, and one draw needn't show every extreme that they name: `segment_for_slot`: each segment appears in exactly one slot.
All inputs are finite; a program needn't handle non-finite values.
Results may differ from a plain program's by a relative error of at most 0.012.
The roundings to bfloat16 on the way count: a program that leaves them out, or rounds other values in their place, can miss the bound.
Values may be sent and summed in bfloat16 or wider, within the bound.
No kernel may reach another device: no remote copies, remote signals or barrier semaphores. Data moves between devices by JAX's collectives and lax.ppermute only.
A program may use at most 64 MiB of HBM per device.

v0:
```python
import jax
import jax.numpy as jnp
from jax import lax
from jax.sharding import PartitionSpec as P

HD = 128
CG = 128
RATE = 4
SLOTS = 2
SEG = 256
MEM = 64


def compress_rows(local_rows, conv_local):
    count_rows, channels = local_rows.shape
    groups = channels // CG
    shaped = local_rows.reshape(count_rows // RATE, RATE, groups, CG)
    kernel = conv_local.reshape(RATE, CG, groups, CG)
    mixed_out = jnp.einsum("mtgc,tcgo->mgo", shaped, kernel, preferred_element_type=jnp.float32)
    return mixed_out.reshape(count_rows // RATE, channels).astype(jnp.bfloat16)


def add_product(source, weight_rows):
    return jnp.dot(source, weight_rows, preferred_element_type=jnp.float32)


def local_attention(queries, keys_here, values_here):
    total_rows, head_count, head_dim = queries.shape
    slot_count = total_rows // SEG
    shaped_q = queries.reshape(slot_count, SEG, head_count, head_dim)
    shaped_k = keys_here.reshape(slot_count, SEG, head_count, head_dim)
    shaped_v = values_here.reshape(slot_count, SEG, head_count, head_dim)
    scores = jnp.einsum(
        "asnd,atnd->asnt", shaped_q, shaped_k, preferred_element_type=jnp.float32
    ) * HD ** (-0.5)
    causal = jnp.arange(SEG, dtype=jnp.int32)[:, None] >= jnp.arange(SEG, dtype=jnp.int32)[None, :]
    scores = jnp.where(causal[None, :, None, :], scores, -jnp.inf)
    row_best = jnp.max(scores, axis=3)
    weights = jnp.exp(scores - row_best[..., None])
    denominator = jnp.sum(weights, axis=3)
    weighted_numerator = jnp.einsum(
        "asnt,atnd->asnd",
        weights.astype(jnp.bfloat16),
        shaped_v,
        preferred_element_type=jnp.float32,
    )
    return (
        row_best.reshape(total_rows, head_count),
        denominator.reshape(total_rows, head_count),
        weighted_numerator.reshape(total_rows, head_count, head_dim),
    )


def memory_step(state, pieces, queries, row_segment, segment_for_slot):
    keys_in, values_in = pieces
    count_keys = keys_in.shape[0]
    total_rows, head_count, head_dim = queries.shape
    key_slot = jnp.arange(count_keys, dtype=jnp.int32) // MEM
    slot_ids = jnp.arange(segment_for_slot.shape[0], dtype=jnp.int32)
    key_segment = jnp.sum(
        jnp.where(key_slot[:, None] == slot_ids[None, :], segment_for_slot[None, :], 0), axis=1
    )
    row_best, denominator, weighted_numerator = state
    shaped_keys = keys_in.reshape(count_keys, head_count, head_dim)
    shaped_values = values_in.reshape(count_keys, head_count, head_dim)
    scores = jnp.einsum(
        "rnd,knd->rnk", queries, shaped_keys, preferred_element_type=jnp.float32
    ) * HD ** (-0.5)
    allowed = key_segment[None, None, :] < row_segment[:, None, None]
    scores = jnp.where(allowed, scores, -jnp.inf)
    new_best = jnp.maximum(row_best, jnp.max(scores, axis=2))
    weights = jnp.exp(scores - new_best[:, :, None])
    factor = jnp.exp(row_best - new_best)
    denominator = denominator * factor + jnp.sum(weights, axis=2)
    weighted_numerator = weighted_numerator * factor[:, :, None] + jnp.einsum(
        "rnk,knd->rnd",
        weights.astype(jnp.bfloat16),
        shaped_values,
        preferred_element_type=jnp.float32,
    )
    return (new_best, denominator, weighted_numerator)


def on_device(
    activations, conv_weight, query_weight, key_weight, value_weight, segment_for_slot, book_length
):
    compressed_local = compress_rows(activations, conv_weight)
    full_rows, full_compressed = (
        lax.all_gather(activations, ("tensor", "sub"), axis=1, tiled=True),
        lax.all_gather(compressed_local, ("tensor", "sub"), axis=1, tiled=True),
    )
    total_rows = full_rows.shape[0]
    local_width = query_weight.shape[1]
    head_count = local_width // HD
    shard_index = lax.axis_index("seq")
    my_segments = lax.dynamic_slice_in_dim(segment_for_slot, shard_index * SLOTS, SLOTS, 0)
    row_segment = jnp.repeat(my_segments, SEG, total_repeat_length=total_rows)
    query_rows = lax.all_gather(query_weight, "seq", axis=0, tiled=True)
    key_matrix_rows = lax.all_gather(key_weight, "seq", axis=0, tiled=True)
    value_rows = lax.all_gather(value_weight, "seq", axis=0, tiled=True)
    queries = add_product(full_rows, query_rows).astype(jnp.bfloat16)
    keys_here = add_product(full_rows, key_matrix_rows).astype(jnp.bfloat16)
    values_here = add_product(full_rows, value_rows).astype(jnp.bfloat16)
    keys_mem = add_product(full_compressed, key_matrix_rows).astype(jnp.bfloat16)
    values_mem = add_product(full_compressed, value_rows).astype(jnp.bfloat16)
    shaped_q = queries.reshape(total_rows, head_count, HD)
    state = local_attention(
        shaped_q,
        keys_here.reshape(total_rows, head_count, HD),
        values_here.reshape(total_rows, head_count, HD),
    )
    state = memory_step(
        state,
        (
            lax.all_gather(keys_mem, "seq", axis=0, tiled=True),
            lax.all_gather(values_mem, "seq", axis=0, tiled=True),
        ),
        shaped_q,
        row_segment,
        segment_for_slot,
    )
    row_best, denominator, weighted_numerator = state
    result = (weighted_numerator / denominator[:, :, None]).reshape(total_rows, local_width)
    position = row_segment * SEG + jnp.arange(total_rows, dtype=jnp.int32) % SEG
    result = jnp.where((position < book_length[0])[:, None], result, 0.0)
    return result.astype(jnp.bfloat16)


def solution(mesh):
    placed = (
        P(("groups", "seq"), ("tensor", "sub")),
        P(None, ("tensor", "sub")),
        P("seq", ("tensor", "sub")),
        P("seq", ("tensor", "sub")),
        P("seq", ("tensor", "sub")),
        P("groups"),
        P("groups"),
    )
    return jax.shard_map(
        on_device,
        mesh=mesh,
        in_specs=placed,
        out_specs=P(("groups", "seq"), ("tensor", "sub")),
        check_vma=False,
    )
```

profile of v0, /device:TPU:0, one launch (start us, length us, event | category | flops | bytes accessed | tf_op | source)
XLA Modules:
  0.0 350.5 jit_solution(3054702752094949203)
XLA Ops:
  6.5 0.0 copy-start
  6.5 0.0 all-gather.6.cloned.1.call-start
  6.5 0.7 all-gather.6.cloned.1.call-update
  7.3 0.0 all-gather.10.cloned.1.call-start
  7.3 0.7 all-gather.10.cloned.1.call-update
  8.0 0.0 all-gather.12.cloned.1.call-start
  8.1 0.7 all-gather.12.cloned.1.call-update
  8.7 0.0 all-gather.14.cloned.1.call-start
  8.8 0.0 copy-start.5
  8.8 0.0 copy-start.4
  8.8 1.5 copy.64
  10.3 0.0 copy-done
  10.3 0.3 copy.65
  10.6 1.7 fusion.17
  12.3 0.0 all-gather.14.cloned.1.call-update
  12.3 0.0 all-gather.8.cloned.1.call-start
  12.4 0.5 all-gather.8.cloned.1.call-update
  13.5 0.0 copy-done.5
  13.6 0.1 dynamic_slice.3
  13.6 0.6 fusion.41
  14.2 0.1 select_reduce_fusion
  14.3 0.0 copy-done.4
  14.3 1.3 fusion.32
  15.6 1.3 broadcast_select_fusion
  16.9 0.2 broadcast_compare_fusion
  17.1 29.0 %all-gather.6.cloned.1.call-done = bf16[512,4096]{1,0:T(8,128)(2,1)} async-done(((bf16[512,1024]{1,0:T(8,128)(2,1)}), bf16[512,4096]{1,0:T(8,128)(2,1)}) %all-gather.6.cloned.1.call-update) | async-done | bytes 4194320 | tf_op jit(solution)/shard_map/all_gather | solution.py:89
  46.1 82.4 %all-gather.10.cloned.1.call-done = bf16[4096,512]{1,0:T(8,128)(2,1)} async-done(((bf16[1024,512]{1,0:T(8,128)(2,1)}), bf16[4096,512]{1,0:T(8,128)(2,1)}) %all-gather.10.cloned.1.call-update) | async-done | bytes 4194320 | tf_op jit(solution)/shard_map/all_gather | solution.py:99
  128.5 5.8 %convolution_convert_fusion.1 = bf16[512,512]{1,0:T(8,128)(2,1)S(1)} fusion(bf16[512,4096]{1,0:T(8,128)(2,1)} %all-gather.6.cloned.1.call-done, bf16[4096,512]{1,0:T(8,128)(2,1)} %all-gather.10.cloned.1.call-done), kind=kOutput, calls=%fused_computation.18 | convolution fusion | flops 2147745792 | bytes 8912896 | tf_op jit(solution)/shard_map/dot_general | solution.py:24
  134.3 0.1 reshape_reshape.10
  134.4 75.0 %all-gather.12.cloned.1.call-done = bf16[4096,512]{1,0:T(8,128)(2,1)} async-done(((bf16[1024,512]{1,0:T(8,128)(2,1)}), bf16[4096,512]{1,0:T(8,128)(2,1)}) %all-gather.12.cloned.1.call-update) | async-done | bytes 4194320 | tf_op jit(solution)/shard_map/all_gather | solution.py:98
  209.4 5.8 %convolution_convert_fusion = bf16[512,512]{0,1:T(8,128)(2,1)S(1)} fusion(bf16[512,4096]{1,0:T(8,128)(2,1)} %all-gather.6.cloned.1.call-done, bf16[4096,512]{1,0:T(8,128)(2,1)} %all-gather.12.cloned.1.call-done), kind=kOutput, calls=%fused_computation.17 | convolution fusion | flops 2147745792 | bytes 8912896 | tf_op jit(solution)/shard_map/dot_general | solution.py:24
  215.2 0.0 copy-start.3
  215.3 0.1 reshape_reshape.11
  215.4 10.7 %all-gather.14.cloned.1.call-done = bf16[128,4096]{0,1:T(8,128)(2,1)} async-done(((bf16[128,1024]{0,1:T(8,128)(2,1)}), bf16[128,4096]{0,1:T(8,128)(2,1)}) %all-gather.14.cloned.1.call-update) | async-done | bytes 1048592 | tf_op jit(solution)/shard_map/all_gather | solution.py:90
  226.1 3.3 convolution_convert_fusion.4
  229.4 21.4 %all_gather.26 = bf16[512,512]{1,0:T(8,128)(2,1)} all-gather(bf16[128,512]{1,0:T(8,128)(2,1)S(1)} %convolution_convert_fusion.4), channel_id=1, replica_groups=mesh['groups'=2,'seq'=4,'tensor'=2,'sub'=2] {'seq'}, dimensions={0}, use_global_device_ids=true | all-gather | bytes 655360 | tf_op jit(solution)/shard_map/all_gather | solution.py:115
  250.8 61.4 %all-gather.8.cloned.1.call-done = bf16[4096,512]{1,0:T(8,128)(2,1)} async-done(((bf16[1024,512]{1,0:T(8,128)(2,1)}), bf16[4096,512]{1,0:T(8,128)(2,1)}) %all-gather.8.cloned.1.call-update) | async-done | bytes 4194320 | tf_op jit(solution)/shard_map/all_gather | solution.py:100
  312.2 0.0 copy-done.3
  312.2 5.8 %convolution_convert_fusion.2 = bf16[512,512]{1,0:T(8,128)(2,1)S(1)} fusion(bf16[512,4096]{1,0:T(8,128)(2,1)} %all-gather.6.cloned.1.call-done, bf16[4096,512]{1,0:T(8,128)(2,1)} %all-gather.8.cloned.1.call-done), kind=kOutput, calls=%fused_computation.19 | convolution fusion | flops 2147745792 | bytes 8912896 | tf_op jit(solution)/shard_map/dot_general | solution.py:24
  318.0 0.1 reshape_reshape.9
  318.1 0.5 fusion.42
  318.6 0.3 fusion.9
  318.9 0.0 copy-start.1
  318.9 0.5 convolution_bitcast_fusion
  319.4 0.3 copy.49
  319.7 0.3 copy.54
  320.1 0.0 copy-done.1
  320.1 0.0 copy-start.2
  320.1 3.0 convolution_convert_fusion.3
  323.1 15.2 %all_gather.27 = bf16[512,512]{1,0:T(8,128)(2,1)S(1)} all-gather(bf16[128,512]{1,0:T(8,128)(2,1)S(1)} %convolution_convert_fusion.3), channel_id=1, replica_groups=mesh['groups'=2,'seq'=4,'tensor'=2,'sub'=2] {'seq'}, dimensions={0}, use_global_device_ids=true | all-gather | bytes 655360 | tf_op jit(solution)/shard_map/all_gather | solution.py:116
  338.4 0.2 copy.62
  338.6 0.0 copy-done.2
  338.6 1.9 fusion.2
  340.5 0.9 fusion
  341.4 1.4 fusion.22
  342.8 0.2 copy.57
  343.0 1.0 select_convert_fusion
  (4 shorter events, 0.0 us)
Async XLA Ops:
  6.5 3.8 %copy-start = (bf16[512,1024]{1,0:T(8,128)(2,1)S(1)}, bf16[512,1024]{1,0:T(8,128)(2,1)}, u32[]{:S(2)}) copy-start(bf16[512,1024]{1,0:T(8,128)(2,1)} %param.9) | copy-start | bytes 3145732
  6.5 39.6 %all-gather.6.cloned.1.call-start = ((), (), s32[]{:S(2)}) async-start(), calls=%async_computation | async-start | bytes 5242880 | tf_op jit(solution)/shard_map/all_gather | solution.py:89
  7.3 121.2 %all-gather.10.cloned.1.call-start = ((), (), s32[]{:S(2)}) async-start(), calls=%async_computation.2 | async-start | bytes 5242880 | tf_op jit(solution)/shard_map/all_gather | solution.py:99
  8.0 201.4 %all-gather.12.cloned.1.call-start = ((), (), s32[]{:S(2)}) async-start(), calls=%async_computation.3 | async-start | bytes 5242880 | tf_op jit(solution)/shard_map/all_gather | solution.py:98
  8.7 217.4 %all-gather.14.cloned.1.call-start = ((), (), s32[]{:S(2)}) async-start(), calls=%async_computation.4 | async-start | bytes 1310720 | tf_op jit(solution)/shard_map/all_gather | solution.py:90
  8.8 4.8 %copy-start.5 = (s32[8]{0:T(128)S(1)}, s32[8]{0:T(128)}, u32[]{:S(2)}) copy-start(s32[8]{0:T(128)} %param.14) | copy-start | bytes 100
  8.8 5.5 %copy-start.4 = (pred[512]{0:T(512)(128)(4,1)S(1)}, pred[512]{0:T(512)(128)(4,1)}, u32[]{:S(2)}) copy-start(pred[512]{0:T(512)(128)(4,1)} %constant.157) | copy-start | bytes 1540
  12.3 299.9 %all-gather.8.cloned.1.call-start = ((), (), s32[]{:S(2)}) async-start(), calls=%async_computation.1 | async-start | bytes 5242880 | tf_op jit(solution)/shard_map/all_gather | solution.py:100
  215.2 96.9 %copy-start.3 = (bf16[512,512]{0,1:T(8,128)(2,1)}, bf16[512,512]{0,1:T(8,128)(2,1)S(1)}, u32[]{:S(2)}) copy-start(bf16[512,512]{0,1:T(8,128)(2,1)S(1)} %convolution_convert_fusion) | copy-start | bytes 1572868
  318.9 1.2 copy-start.1
  320.1 18.4 %copy-start.2 = (bf16[512,512]{1,0:T(8,128)(2,1)S(1)}, bf16[512,512]{1,0:T(8,128)(2,1)}, u32[]{:S(2)}) copy-start(bf16[512,512]{1,0:T(8,128)(2,1)} %all_gather.26) | copy-start | bytes 1572868
Sparse Core Ops, SparseCore 0:
  8.9 37.1 all-gather.5
  47.7 80.7 all-gather.9
  130.1 79.2 all-gather.11
  210.8 15.2 all-gather.13
  227.5 84.6 all-gather.7
where the time goes:
time: 351 us
  waiting for transfers between devices  261 us (74%)
  blocking collectives  36.6 us (10%)
  matrix products  29.6 us (8%)
  between operations  14 us (4%)
  other arithmetic  5.11 us (1%)
  local copies, waits for them, and re-layouts  3.95 us (1%)
    all_gather x1, waiting for transfers between devices, on_device(): key_matrix_rows = lax.all_gather(key_weight, 'seq', axis=0, tiled=True)  82.4 us
    all_gather x1, waiting for transfers between devices, on_device(): query_rows = lax.all_gather(query_weight, 'seq', axis=0, tiled=True)  75 us
    all_gather x1, waiting for transfers between devices, on_device(): value_rows = lax.all_gather(value_weight, 'seq', axis=0, tiled=True)  61.4 us
    all_gather x1, waiting for transfers between devices, on_device(): lax.all_gather(activations, ('tensor', 'sub'), axis=1, tiled=True)  29 us
    dot_general x5, matrix products, add_product(): return jnp.dot(source, weight_rows, preferred_element_type=jnp.float32)  23.6 us
    all_gather x1, blocking collectives, on_device(): lax.all_gather(keys_mem, 'seq', axis=0, tiled=True)  21.4 us
    all_gather x1, blocking collectives, on_device(): lax.all_gather(values_mem, 'seq', axis=0, tiled=True)  15.2 us
    all_gather x1, waiting for transfers between devices, on_device(): lax.all_gather(compressed_local, ('tensor', 'sub'), axis=1, tiled=True)  10.7 us
  transfers between devices with their start and end apart: 5, of which 5 were waited for; matrix products, arithmetic and copies ran while one was open for 6% of the time, Pallas kernels for 0%

commit v1 on v0

--- a/solution.py
+++ b/solution.py
@@ -96,7 +96,14 @@
     my_segments = lax.dynamic_slice_in_dim(segment_for_slot, shard_index * SLOTS, SLOTS, 0)
     row_segment = jnp.repeat(my_segments, SEG, total_repeat_length=total_rows)
     query_rows = lax.all_gather(query_weight, "seq", axis=0, tiled=True)
-    key_matrix_rows = lax.all_gather(key_weight, "seq", axis=0, tiled=True)
+    size = lax.axis_size("seq")
+    route = [(i, (i + 1) % size) for i in range(size)]
+    parts = [key_weight]
+    for far in range(1, size):
+        parts = [lax.ppermute(parts[0], "seq", route), *parts]
+    whole = jnp.concatenate(parts, axis=0)
+    shift = (lax.axis_index("seq") + 1) * parts[-1].shape[0]
+    key_matrix_rows = jnp.roll(whole, shift, axis=0)
     value_rows = lax.all_gather(value_weight, "seq", axis=0, tiled=True)
     queries = add_product(full_rows, query_rows).astype(jnp.bfloat16)
     keys_here = add_product(full_rows, key_matrix_rows).astype(jnp.bfloat16)

time: 351 us -> 290 us (0.83)
  waiting for transfers between devices: 261 us -> 179 us
  local copies, waits for them, and re-layouts: 3.95 us -> 16.2 us
  blocking collectives: 36.6 us -> 42.3 us
    ppermute x0 -> x3, waiting for transfers between devices: none -> 86.7 us  [on_device(): parts = [lax.ppermute(parts[0], 'seq', route), *parts]]
    all_gather x1 -> x0, waiting for transfers between devices: 82.4 us -> none  [on_device(): key_matrix_rows = lax.all_gather(key_weight, 'seq', axis=0, tiled=True)]
    all_gather x1, waiting for transfers between devices: 75 us -> 15.8 us  [on_device(): query_rows = lax.all_gather(query_weight, 'seq', axis=0, tiled=True)]
    all_gather x1, waiting for transfers between devices: 29 us -> 0.01 us  [on_device(): lax.all_gather(activations, ('tensor', 'sub'), axis=1, tiled=True)]
    all_gather x1, waiting for transfers between devices: 61.4 us -> 74.2 us  [on_device(): value_rows = lax.all_gather(value_weight, 'seq', axis=0, tiled=True)]
    unnamed x14 -> x21, local copies, waits for them, and re-layouts: 1.83 us -> 13 us
    all_gather x1, waiting for transfers between devices: 10.7 us -> 0.01 us  [on_device(): lax.all_gather(compressed_local, ('tensor', 'sub'), axis=1, tiled=True)]
    all_gather x1, blocking collectives: 21.4 us -> 26 us  [on_device(): lax.all_gather(keys_mem, 'seq', axis=0, tiled=True)]
  transfers between devices with their start and end apart: 5 -> 7, of which waited for: 5 -> 5; matrix products, arithmetic and copies ran while one was open for 6% -> 10% of each run, Pallas kernels for 0% -> 0%
where the time goes in v1:
time: 290 us; the launch traced here: 289 us
  waiting for transfers between devices  179 us (62%)
  blocking collectives  42.3 us (15%)
  matrix products  29.7 us (10%)
  local copies, waits for them, and re-layouts  16.2 us (6%)
  between operations  14 us (5%)
  other arithmetic  5.07 us (2%)
  starting transfers between devices  3.2 us (1%)
    ppermute x3, waiting for transfers between devices, on_device(): parts = [lax.ppermute(parts[0], 'seq', route), *parts]  86.7 us
    all_gather x1, waiting for transfers between devices, on_device(): value_rows = lax.all_gather(value_weight, 'seq', axis=0, tiled=True)  74.2 us
    all_gather x1, blocking collectives, on_device(): lax.all_gather(keys_mem, 'seq', axis=0, tiled=True)  26 us
    dot_general x5, matrix products, add_product(): return jnp.dot(source, weight_rows, preferred_element_type=jnp.float32)  23.7 us
    all_gather x1, blocking collectives, on_device(): lax.all_gather(values_mem, 'seq', axis=0, tiled=True)  16.4 us
    all_gather x1, waiting for transfers between devices, on_device(): query_rows = lax.all_gather(query_weight, 'seq', axis=0, tiled=True)  15.8 us
    unnamed x21, local copies, waits for them, and re-layouts  13 us
  transfers between devices with their start and end apart: 7, of which 5 were waited for; matrix products, arithmetic and copies ran while one was open for 10% of the time, Pallas kernels for 0%

profile of v1, /device:TPU:0, one launch (start us, length us, event | category | flops | bytes accessed | tf_op | source)
XLA Modules:
  0.0 289.1 jit_solution(17182461577292243757)
XLA Ops:
  6.5 0.0 all-gather.11.cloned.1.call-start
  6.5 1.5 copy.64
  8.0 0.0 copy-start
  8.0 0.0 copy-start.5
  8.1 0.0 copy-start.4
  8.1 1.6 copy.65
  9.7 1.7 fusion.27
  11.3 0.0 all-gather.11.cloned.1.call-update
  11.3 0.0 all-gather.5.cloned.1.call-start
  11.4 0.7 all-gather.5.cloned.1.call-update
  12.1 0.0 all-gather.9.cloned.1.call-start
  12.1 0.7 all-gather.9.cloned.1.call-update
  12.8 0.0 all-gather.7.cloned.1.call-start
  12.9 0.5 all-gather.7.cloned.1.call-update
  13.4 0.0 copy-done
  13.4 3.1 %collective-permute-start = (bf16[1024,512]{1,0:T(8,128)(2,1)S(1)}, bf16[1024,512]{1,0:T(8,128)(2,1)S(1)}, u32[]{:S(2)}, u32[]{:S(2)}) collective-permute-start(bf16[1024,512]{1,0:T(8,128)(2,1)S(1)} %copy-done), channel_id=1, source_target_pairs={{0,4},{4,8},{8,12},{12,0},{1,5},{5,9},{9,13},{13,1},{2,6},{6,10},{... | collective-permute-start | bytes 3145736 | tf_op jit(solution)/shard_map/ppermute | solution.py:103
  16.5 25.2 %collective-permute-done = bf16[1024,512]{1,0:T(8,128)(2,1)S(1)} collective-permute-done((bf16[1024,512]{1,0:T(8,128)(2,1)S(1)}, bf16[1024,512]{1,0:T(8,128)(2,1)S(1)}, u32[]{:S(2)}, u32[]{:S(2)}) %collective-permute-start) | collective-permute-done | bytes 1048608 | tf_op jit(solution)/shard_map/ppermute | solution.py:103
  41.7 0.0 collective-permute-start.1
  41.7 26.1 %collective-permute-done.1 = bf16[1024,512]{1,0:T(8,128)(2,1)S(1)} collective-permute-done((bf16[1024,512]{1,0:T(8,128)(2,1)S(1)}, bf16[1024,512]{1,0:T(8,128)(2,1)S(1)}, u32[]{:S(2)}, u32[]{:S(2)}) %collective-permute-start.1) | collective-permute-done | bytes 1048608 | tf_op jit(solution)/shard_map/ppermute | solution.py:103
  67.8 0.0 collective-permute-start.2
  68.5 0.0 copy-done.5
  68.5 0.1 dynamic_slice.7
  68.6 0.6 fusion.56
  69.2 0.1 select_reduce_fusion
  69.3 0.0 copy-done.4
  69.3 1.3 fusion.45
  70.6 1.3 broadcast_select_fusion
  71.8 0.2 broadcast_compare_fusion
  72.1 35.3 %collective-permute-done.2 = bf16[1024,512]{1,0:T(8,128)(2,1)} collective-permute-done((bf16[1024,512]{1,0:T(8,128)(2,1)S(1)}, bf16[1024,512]{1,0:T(8,128)(2,1)}, u32[]{:S(2)}, u32[]{:S(2)}) %collective-permute-start.2) | collective-permute-done | bytes 1048608 | tf_op jit(solution)/shard_map/ppermute | solution.py:103
  107.4 2.3 constant_dynamic-update-slice_fusion.7
  109.7 1.1 constant_dynamic-update-slice_fusion.6
  110.8 1.1 constant_dynamic-update-slice_fusion.5
  111.8 1.1 constant_dynamic-update-slice_fusion.4
  112.9 2.3 constant_dynamic-update-slice_fusion.3
  115.1 1.1 constant_dynamic-update-slice_fusion.2
  116.2 1.1 constant_dynamic-update-slice_fusion.1
  117.3 1.1 constant_dynamic-update-slice_fusion
  118.3 3.3 %fusion.28 = bf16[128,512]{1,0:T(8,128)(2,1)S(1)} fusion(bf16[128,4096]{0,1:T(8,128)(2,1)} %all-gather.11.cloned.1.call-done, bf16[8192,512]{1,0:T(8,128)(2,1)} %constant_dynamic-update-slice_fusion, s32[]{:T(128)S(6)} %select_n.84), kind=kOutput, calls=%fused_computation.27 | convolution fusion | flops 536936448 | bytes 5373956 | tf_op jit(solution)/shard_map/dot_general | solution.py:24
  121.6 26.0 %all_gather.22 = bf16[512,512]{1,0:T(8,128)(2,1)} all-gather(bf16[128,512]{1,0:T(8,128)(2,1)S(1)} %fusion.28), channel_id=1, replica_groups=mesh['groups'=2,'seq'=4,'tensor'=2,'sub'=2] {'seq'}, dimensions={0}, use_global_device_ids=true | all-gather | bytes 655360 | tf_op jit(solution)/shard_map/all_gather | solution.py:122
  147.6 5.8 %fusion.24 = bf16[512,512]{0,1:T(8,128)(2,1)S(1)} fusion(bf16[512,4096]{1,0:T(8,128)(2,1)} %all-gather.5.cloned.1.call-done, bf16[8192,512]{1,0:T(8,128)(2,1)} %constant_dynamic-update-slice_fusion, s32[]{:T(128)S(6)} %select_n.84), kind=kOutput, calls=%fused_computation.25 | convolution fusion | flops 2147745792 | bytes 8912900 | tf_op jit(solution)/shard_map/dot_general | solution.py:24
  153.5 0.1 reshape_reshape.10
  153.6 15.8 %all-gather.9.cloned.1.call-done = bf16[4096,512]{1,0:T(8,128)(2,1)} async-done(((bf16[1024,512]{1,0:T(8,128)(2,1)}), bf16[4096,512]{1,0:T(8,128)(2,1)}) %all-gather.9.cloned.1.call-update) | async-done | bytes 4194320 | tf_op jit(solution)/shard_map/all_gather | solution.py:98
  169.4 5.8 %convolution_convert_fusion = bf16[512,512]{0,1:T(8,128)(2,1)S(1)} fusion(bf16[512,4096]{1,0:T(8,128)(2,1)} %all-gather.5.cloned.1.call-done, bf16[4096,512]{1,0:T(8,128)(2,1)} %all-gather.9.cloned.1.call-done), kind=kOutput, calls=%fused_computation.22 | convolution fusion | flops 2147745792 | bytes 8912896 | tf_op jit(solution)/shard_map/dot_general | solution.py:24
  175.2 0.0 copy-start.3
  175.3 0.1 reshape_reshape.11
  175.4 74.2 %all-gather.7.cloned.1.call-done = bf16[4096,512]{1,0:T(8,128)(2,1)} async-done(((bf16[1024,512]{1,0:T(8,128)(2,1)}), bf16[4096,512]{1,0:T(8,128)(2,1)}) %all-gather.7.cloned.1.call-update) | async-done | bytes 4194320 | tf_op jit(solution)/shard_map/all_gather | solution.py:107
  249.6 0.0 copy-done.3
  249.6 5.8 %convolution_convert_fusion.1 = bf16[512,512]{1,0:T(8,128)(2,1)S(1)} fusion(bf16[512,4096]{1,0:T(8,128)(2,1)} %all-gather.5.cloned.1.call-done, bf16[4096,512]{1,0:T(8,128)(2,1)} %all-gather.7.cloned.1.call-done), kind=kOutput, calls=%fused_computation.23 | convolution fusion | flops 2147745792 | bytes 8912896 | tf_op jit(solution)/shard_map/dot_general | solution.py:24
  255.4 0.1 reshape_reshape.9
  255.5 0.5 fusion.57
  256.1 0.3 fusion.13
  256.4 0.0 copy-start.1
  256.4 0.5 convolution_bitcast_fusion
  256.9 0.3 copy.49
  257.2 0.3 copy.54
  257.6 0.0 copy-done.1
  257.6 3.0 %convolution_convert_fusion.2 = bf16[128,512]{1,0:T(8,128)(2,1)S(1)} fusion(bf16[128,4096]{0,1:T(8,128)(2,1)S(1)} %copy-done.1, bf16[4096,512]{1,0:T(8,128)(2,1)} %all-gather.7.cloned.1.call-done), kind=kOutput, calls=%fused_computation.28 | convolution fusion | flops 536936448 | bytes 5373952 | tf_op jit(solution)/shard_map/dot_general | solution.py:24
  260.6 16.4 %all_gather.23 = bf16[512,512]{1,0:T(8,128)(2,1)S(1)} all-gather(bf16[128,512]{1,0:T(8,128)(2,1)S(1)} %convolution_convert_fusion.2), channel_id=1, replica_groups=mesh['groups'=2,'seq'=4,'tensor'=2,'sub'=2] {'seq'}, dimensions={0}, use_global_device_ids=true | all-gather | bytes 655360 | tf_op jit(solution)/shard_map/all_gather | solution.py:123
  277.0 0.2 copy.62
  277.2 1.9 fusion.6
  279.1 0.9 fusion
  280.0 1.4 fusion.35
  281.4 0.2 copy.57
  281.6 1.0 select_convert_fusion
  (8 shorter events, 0.1 us)
Async XLA Ops:
  6.5 111.8 %all-gather.11.cloned.1.call-start = ((), (), s32[]{:S(2)}) async-start(), calls=%async_computation.3 | async-start | bytes 1310720 | tf_op jit(solution)/shard_map/all_gather | solution.py:90
  8.0 5.4 %copy-start = (bf16[1024,512]{1,0:T(8,128)(2,1)S(1)}, bf16[1024,512]{1,0:T(8,128)(2,1)}, u32[]{:S(2)}) copy-start(bf16[1024,512]{1,0:T(8,128)(2,1)} %param.12) | copy-start | bytes 3145732
  8.0 60.4 %copy-start.5 = (s32[8]{0:T(128)S(1)}, s32[8]{0:T(128)}, u32[]{:S(2)}) copy-start(s32[8]{0:T(128)} %param.14) | copy-start | bytes 100
  8.1 61.2 %copy-start.4 = (pred[512]{0:T(512)(128)(4,1)S(1)}, pred[512]{0:T(512)(128)(4,1)}, u32[]{:S(2)}) copy-start(pred[512]{0:T(512)(128)(4,1)} %constant.181) | copy-start | bytes 1540
  11.3 136.3 %all-gather.5.cloned.1.call-start = ((), (), s32[]{:S(2)}) async-start(), calls=%async_computation | async-start | bytes 5242880 | tf_op jit(solution)/shard_map/all_gather | solution.py:89
  12.1 157.3 %all-gather.9.cloned.1.call-start = ((), (), s32[]{:S(2)}) async-start(), calls=%async_computation.2 | async-start | bytes 5242880 | tf_op jit(solution)/shard_map/all_gather | solution.py:98
  12.8 236.8 %all-gather.7.cloned.1.call-start = ((), (), s32[]{:S(2)}) async-start(), calls=%async_computation.1 | async-start | bytes 5242880 | tf_op jit(solution)/shard_map/all_gather | solution.py:107
  13.4 28.3 %collective-permute-start = (bf16[1024,512]{1,0:T(8,128)(2,1)S(1)}, bf16[1024,512]{1,0:T(8,128)(2,1)S(1)}, u32[]{:S(2)}, u32[]{:S(2)}) collective-permute-start(bf16[1024,512]{1,0:T(8,128)(2,1)S(1)} %copy-done), channel_id=1, source_target_pairs={{0,4},{4,8},{8,12},{12,0},{1,5},{5,9},{9,13},{13,1},{2,6},{6,10},{... | collective-permute-start | bytes 3145736 | tf_op jit(solution)/shard_map/ppermute | solution.py:103
  41.7 26.1 %collective-permute-start.1 = (bf16[1024,512]{1,0:T(8,128)(2,1)S(1)}, bf16[1024,512]{1,0:T(8,128)(2,1)S(1)}, u32[]{:S(2)}, u32[]{:S(2)}) collective-permute-start(bf16[1024,512]{1,0:T(8,128)(2,1)S(1)} %collective-permute-done), channel_id=1, source_target_pairs={{0,4},{4,8},{8,12},{12,0},{1,5},{5,9},{9,13},{13,1},{2,6},{6,10},{... | collective-permute-start | bytes 3145736 | tf_op jit(solution)/shard_map/ppermute | solution.py:103
  67.8 39.6 %collective-permute-start.2 = (bf16[1024,512]{1,0:T(8,128)(2,1)S(1)}, bf16[1024,512]{1,0:T(8,128)(2,1)}, u32[]{:S(2)}, u32[]{:S(2)}) collective-permute-start(bf16[1024,512]{1,0:T(8,128)(2,1)S(1)} %collective-permute-done.1), channel_id=1, source_target_pairs={{0,4},{4,8},{8,12},{12,0},{1,5},{5,9},{9,13},{13,1},{2,6},{6,10},{... | collective-permute-start | bytes 3145736 | tf_op jit(solution)/shard_map/ppermute | solution.py:103
  175.2 74.4 %copy-start.3 = (bf16[512,512]{0,1:T(8,128)(2,1)}, bf16[512,512]{0,1:T(8,128)(2,1)S(1)}, u32[]{:S(2)}) copy-start(bf16[512,512]{0,1:T(8,128)(2,1)S(1)} %convolution_convert_fusion) | copy-start | bytes 1572868
  256.4 1.2 copy-start.1
  257.6 19.6 %copy-start.2 = (bf16[512,512]{1,0:T(8,128)(2,1)S(1)}, bf16[512,512]{1,0:T(8,128)(2,1)}, u32[]{:S(2)}) copy-start(bf16[512,512]{1,0:T(8,128)(2,1)} %all_gather.22) | copy-start | bytes 1572868
Sparse Core Ops, SparseCore 0:
  11.5 19.4 all-gather.10
  32.5 34.4 all-gather.4
  68.6 100.7 all-gather.8
  170.8 78.7 all-gather.6
